TPU v7x, 256 devices: a whole 4x4x8 slice. The times are simulated.
256 devices in a mesh: cuts: 32 (over z_lo, y, core), coil: 8 (over z_hi, x).
Axes of the slice: x: 4, y: 4, z: 8 (z_hi: 2, z_lo: 4; z = z_hi * 4 + z_lo), core: 2. Of those that a mesh axis runs over, the one named last changes fastest.
Arguments:
- volume: bfloat16 [2, 256, 256, 256], P(None, 'cuts', 'coil'), may hold values from -6 to 6
- coil_maps: bfloat16 [16, 2, 256, 256, 256], P('coil', None, 'cuts'), may hold values from -3 to 3
- kspace: bfloat16 [16, 2, 256, 256, 256], P('coil', None, None, 'cuts'), may hold values from -3 to 3
- line_mask: int32 [256, 256], replicated, may hold values 0 or 1
Outputs:
- updated: bfloat16 [2, 256, 256, 256], P(None, 'coil', 'cuts')
All inputs are finite; a program needn't handle non-finite values.
Results may differ from a plain program's by a relative error of at most 0.012.
Values may be sent and summed in bfloat16 or wider, within the bound.
A program may use at most 128 MiB of HBM per device.

v0:
```python
import functools
import math

import jax
import jax.numpy as jnp
import numpy as np
from jax import lax
from jax.experimental import pallas as pl
from jax.experimental.pallas import tpu as pltpu
from jax.sharding import PartitionSpec as P

MESH = pl.DeviceIdType.MESH
BF16 = jnp.bfloat16
F32 = jnp.float32
N = 256
CUTS = 32
PLANES = 8
GROUPS = 4
XP = PLANES // GROUPS


def tables():
    counter = np.arange(N, dtype=np.int32)
    product = counter[:, None] * counter[None, :] % N
    angles = product.astype(np.float32) * np.float32(2.0 * math.pi / N)
    factor = np.float32(1.0 / math.sqrt(N))
    return (
        (np.cos(angles) * factor).astype(BF16),
        (np.sin(angles) * factor).astype(BF16),
    )


def dot(a, b):
    return jnp.dot(a, b, preferred_element_type=F32)


def kernel(
    vol_in, maps_in, ks_in, mask_in, cos_in, sin_in, out,
    ks, maps, mask, vol, cosv, sinv, fwd, inv, split, merge, hyb, arr, kspc, gsend, rsbuf, psend, fin,
    in_sem, vol_sem, agz_recv, agx_recv, ag_send, a2a_send, a2a_recv, rs_send, rs_recv, mv_send, mv_recv, mv_loc,
):
    me = lax.axis_index("cuts")
    my_coil = lax.axis_index("coil")
    zhi = lax.div(my_coil, 4)
    xpos = lax.rem(my_coil, 4)
    partner = lax.rem(my_coil + 4, 8)
    home = lax.div(me, 4)
    slot = lax.rem(me, 4)

    def load(k, src, dst):
        return pltpu.make_async_copy(src, dst, in_sem.at[k])

    loads = [
        load(0, cos_in, cosv),
        load(1, sin_in, sinv),
        load(2, ks_in.at[0], ks.at[0]),
        load(3, ks_in.at[1], ks.at[1]),
        load(4, mask_in, mask),
        load(5, maps_in, maps),
    ]
    for item in loads:
        item.start()
    my_rows = pl.ds(pl.multiple_of(my_coil * 32, 32), 32)
    vol_own = pltpu.make_async_copy(vol_in, vol.at[:, :, my_rows, :], vol_sem)
    vol_own.start()

    barrier = pltpu.get_barrier_semaphore()

    def greet(a, b):
        pl.semaphore_signal(barrier, inc=1, device_id=(a, b), device_id_type=MESH)

    def greet_cut(k, carry):
        greet(lax.rem(me + k, CUTS), my_coil)
        return carry

    lax.fori_loop(1, CUTS, greet_cut, 0)
    greet(me, partner)
    for d in range(1, 4):
        greet(me, zhi * 4 + lax.rem(xpos + d, 4))
    quarter = lax.div(me, 8)

    def greet_source(k, carry):
        a = my_coil * 4 + lax.rem(k, 4)
        b = lax.div(k, 4) * 4 + quarter

        @pl.when(jnp.logical_or(a != me, b != my_coil))
        def _():
            greet(a, b)

        return carry

    lax.fori_loop(0, 8, greet_source, 0)

    loads[0].wait()
    loads[1].wait()
    c = cosv[...]
    s = sinv[...]
    fwd[:N, :N] = c
    fwd[N:, N:] = c
    fwd[:N, N:] = -s
    fwd[N:, :N] = s
    inv[:N, :N] = c
    inv[N:, N:] = c
    inv[:N, N:] = s
    inv[N:, :N] = -s

    def transform_x(coil):
        for part in range(2):

            def spread(b, carry):
                v = ks[coil, part, pl.ds(pl.multiple_of(b * 32, 32), 32)].astype(F32).reshape(N, N)
                rows = pl.ds(pl.multiple_of(b * N, N), N)
                split[part, 0, rows, :] = v[:, :128]
                split[part, 1, rows, :] = v[:, 128:]
                return carry

            lax.fori_loop(0, 8, spread, 0)

        def line(ky, carry):
            rows = pl.ds(ky, N, stride=8)
            cols = [
                jnp.concatenate([split[0, half, rows, :], split[1, half, rows, :]], axis=0).astype(BF16)
                for half in range(2)
            ]
            r = dot(fwd[...], jnp.concatenate(cols, axis=1))
            for part in range(2):
                for half in range(2):
                    merge[part, half, rows, :] = r[part * N : (part + 1) * N, half * 128 : (half + 1) * 128]
            return carry

        lax.fori_loop(0, 8, line, 0)
        for part in range(2):

            def gather(b, carry):
                rows = pl.ds(pl.multiple_of(b * N, N), N)
                v = jnp.concatenate([merge[part, 0, rows, :], merge[part, 1, rows, :]], axis=1)
                hyb[coil, part, pl.ds(pl.multiple_of(b * 32, 32), 32)] = v.reshape(32, 8, N).astype(BF16)
                return carry

            lax.fori_loop(0, 8, gather, 0)

    def send_slabs(coil, group):
        planes = pl.ds(group * XP, XP)

        def one(k, carry):
            to = lax.rem(me + k, CUTS)
            pltpu.make_async_remote_copy(
                src_ref=hyb.at[coil, :, pl.ds(to * PLANES + group * XP, XP), :, :],
                dst_ref=arr.at[coil, :, planes, me, :, :],
                send_sem=a2a_send.at[group],
                recv_sem=a2a_recv.at[group],
                device_id=(to, my_coil),
                device_id_type=MESH,
            ).start()
            return carry

        lax.fori_loop(1, CUTS, one, 0)
        pltpu.make_async_copy(
            hyb.at[coil, :, pl.ds(me * PLANES + group * XP, XP), :, :],
            arr.at[coil, :, planes, me, :, :],
            a2a_recv.at[group],
        ).start()

    def send_volume(rows, source, peer, recv):
        pltpu.make_async_remote_copy(
            src_ref=source,
            dst_ref=vol.at[:, :, rows, :],
            send_sem=ag_send,
            recv_sem=recv,
            device_id=(me, peer),
            device_id_type=MESH,
        ).start()

    loads[2].wait()
    transform_x(0)
    pl.semaphore_wait(barrier, 43 - self_count(me, my_coil))

    send_volume(my_rows, vol_in, partner, agz_recv)
    for d in range(1, 4):
        send_volume(my_rows, vol_in, zhi * 4 + lax.rem(xpos + d, 4), agx_recv)
    send_slabs(0, 0)
    loads[3].wait()
    transform_x(1)
    send_slabs(1, 0)
    pltpu.make_async_copy(vol_in, vol_in, agz_recv).wait()
    far_rows = pl.ds(pl.multiple_of(partner * 32, 32), 32)
    for d in range(1, 4):
        send_volume(far_rows, vol.at[:, :, far_rows, :], zhi * 4 + lax.rem(xpos + d, 4), agx_recv)
    for group in range(1, GROUPS):
        send_slabs(0, group)
        send_slabs(1, group)

    loads[5].wait()
    vol_own.wait()
    six = vol.at[:, :, pl.ds(0, 192), :]
    pltpu.make_async_copy(six, six, agx_recv).wait()

    def predict(t, carry):
        coil = lax.div(t, PLANES)
        x = lax.rem(t, PLANES)
        vr = vol[0, x].astype(F32)
        vi = vol[1, x].astype(F32)
        mr = maps[coil, 0, x].astype(F32)
        mi = maps[coil, 1, x].astype(F32)
        image = jnp.concatenate([(mr * vr - mi * vi).astype(BF16), (mr * vi + mi * vr).astype(BF16)], axis=1)
        z = dot(image, fwd[...]).astype(BF16)
        kspc[coil, x] = dot(inv[...], jnp.concatenate([z[:, :N], z[:, N:]], axis=0)).astype(BF16)
        return carry

    lax.fori_loop(0, 2 * PLANES, predict, 0)
    loads[4].wait()

    def back(x, carry):
        weight = mask[...].astype(F32)
        gr = None
        for coil in range(2):
            res = []
            for part in range(2):
                k = kspc[coil, x, part * N : (part + 1) * N, :].astype(F32)
                h = arr[coil, part, x].astype(F32).reshape(N, N)
                res.append((weight * (k - h)).astype(BF16))
            y = dot(fwd[...], jnp.concatenate(res, axis=0)).astype(BF16)
            b = dot(jnp.concatenate([y[:N], y[N:]], axis=1), inv[...]).astype(BF16).astype(F32)
            br, bi = b[:, :N], b[:, N:]
            mr = maps[coil, 0, x].astype(F32)
            mi = maps[coil, 1, x].astype(F32)
            tr = mr * br + mi * bi
            ti = mr * bi - mi * br
            gr, gi = (tr, ti) if gr is None else (gr + tr, gi + ti)
        gsend[0, x] = (-0.5 * gr).astype(BF16)
        gsend[1, x] = (-0.5 * gi).astype(BF16)
        return carry

    def send_sums(group):
        planes = pl.ds(group * XP, XP)
        for d in range(1, 4):
            to = lax.rem(xpos + d, 4)
            pltpu.make_async_remote_copy(
                src_ref=gsend.at[:, planes, pl.ds(pl.multiple_of(to * 64, 64), 64), :],
                dst_ref=rsbuf.at[xpos, :, planes, :, :],
                send_sem=rs_send.at[group],
                recv_sem=rs_recv.at[group],
                device_id=(me, zhi * 4 + to),
                device_id_type=MESH,
            ).start()

    lead = (1 - zhi).astype(F32)
    own_rows = pl.ds(pl.multiple_of(xpos * 64, 64), 64)

    def finish_sums(group):
        three = rsbuf.at[pl.ds(0, 3), :, pl.ds(group * XP, XP), :, :]
        pltpu.make_async_copy(three, three, rs_recv.at[group]).wait()

        def one(t, carry):
            part = lax.rem(t, 2)
            x = group * XP + lax.div(t, 2)
            total = lead * vol[part, x, own_rows, :].astype(F32) + gsend[part, x, own_rows, :].astype(F32)
            for d in range(1, 4):
                total += rsbuf[lax.rem(xpos + d, 4), part, x].astype(F32)
            psend[part, x] = total.reshape(8, 8, N).astype(BF16)
            return carry

        lax.fori_loop(0, 2 * XP, one, 0)

        def move(k, carry):
            to = xpos * 8 + k
            src = psend.at[:, pl.ds(group * XP, XP), k, :, :]
            dst = fin.at[zhi, :, pl.ds(slot * PLANES + group * XP, XP), :, :]
            itself = jnp.logical_and(to == me, home == my_coil)

            @pl.when(itself)
            def _():
                pltpu.make_async_copy(src, dst, mv_loc.at[group]).start()

            @pl.when(jnp.logical_not(itself))
            def _():
                pltpu.make_async_remote_copy(
                    src_ref=src,
                    dst_ref=dst,
                    send_sem=mv_send.at[group],
                    recv_sem=mv_recv.at[group],
                    device_id=(to, home),
                    device_id_type=MESH,
                ).start()

            return carry

        lax.fori_loop(0, 8, move, 0)

    for group in range(GROUPS):
        here = arr.at[:, :, pl.ds(group * XP, XP), :, :, :]
        pltpu.make_async_copy(here, here, a2a_recv.at[group]).wait()
        lax.fori_loop(group * XP, (group + 1) * XP, back, 0)
        send_sums(group)
        if group > 0:
            finish_sums(group - 1)
    finish_sums(GROUPS - 1)

    alone = self_count(me, my_coil) == 1
    for group in range(GROUPS):
        full = psend.at[:, pl.ds(group * XP, XP), :, :, :]
        most = psend.at[:, pl.ds(group * XP, XP), pl.ds(0, 7), :, :]
        single = psend.at[:, pl.ds(group * XP, XP), 0, :, :]

        @pl.when(alone)
        def _():
            pltpu.make_async_copy(most, most, mv_recv.at[group]).wait()
            pltpu.make_async_copy(single, single, mv_loc.at[group]).wait()
            pltpu.make_async_copy(most, most, mv_send.at[group]).wait()

        @pl.when(jnp.logical_not(alone))
        def _():
            pltpu.make_async_copy(full, full, mv_recv.at[group]).wait()
            pltpu.make_async_copy(full, full, mv_send.at[group]).wait()

    for part in range(2):
        out[part] = (fin[0, part].astype(F32) + fin[1, part].astype(F32)).astype(BF16)

    for group in range(GROUPS):
        sent = hyb.at[:, :, pl.ds(0, 31 * XP), :, :]
        pltpu.make_async_copy(sent, sent, a2a_send.at[group]).wait()
        three = rsbuf.at[pl.ds(0, 3), :, pl.ds(group * XP, XP), :, :]
        pltpu.make_async_copy(three, three, rs_send.at[group]).wait()
    seven = vol.at[:, :, pl.ds(0, 224), :]
    pltpu.make_async_copy(seven, seven, ag_send).wait()


def self_count(me, my_coil):
    same = jnp.logical_and(lax.div(me, 8) == lax.rem(my_coil, 4), lax.div(me, 4) == my_coil)
    return same.astype(jnp.int32)


def body(volume, coil_maps, kspace, line_mask):
    cos_table, sin_table = tables()
    any_space = pl.BlockSpec(memory_space=pl.ANY)
    dma = pltpu.SemaphoreType.DMA
    return pl.pallas_call(
        kernel,
        out_shape=jax.ShapeDtypeStruct((2, 32, 8, N), BF16),
        in_specs=[any_space] * 6,
        out_specs=pl.BlockSpec(memory_space=pltpu.VMEM),
        scratch_shapes=[
            pltpu.VMEM((2, 2, N, 8, N), BF16),
            pltpu.VMEM((2, 2, PLANES, N, N), BF16),
            pltpu.VMEM((N, N), jnp.int32),
            pltpu.VMEM((2, PLANES, N, N), BF16),
            pltpu.VMEM((N, N), BF16),
            pltpu.VMEM((N, N), BF16),
            pltpu.VMEM((2 * N, 2 * N), BF16),
            pltpu.VMEM((2 * N, 2 * N), BF16),
            pltpu.VMEM((2, 2, 8 * N, 128), F32),
            pltpu.VMEM((2, 2, 8 * N, 128), F32),
            pltpu.VMEM((2, 2, N, 8, N), BF16),
            pltpu.VMEM((2, 2, PLANES, CUTS, 8, N), BF16),
            pltpu.VMEM((2, PLANES, 2 * N, N), BF16),
            pltpu.VMEM((2, PLANES, N, N), BF16),
            pltpu.VMEM((4, 2, PLANES, 64, N), BF16),
            pltpu.VMEM((2, PLANES, 8, 8, N), BF16),
            pltpu.VMEM((2, 2, 32, 8, N), BF16),
            dma((6,)),
            dma,
            dma,
            dma,
            dma,
            dma((GROUPS,)),
            dma((GROUPS,)),
            dma((GROUPS,)),
            dma((GROUPS,)),
            dma((GROUPS,)),
            dma((GROUPS,)),
            dma((GROUPS,)),
        ],
        compiler_params=pltpu.CompilerParams(
            collective_id=0, has_side_effects=True, vmem_limit_bytes=60 * 1024 * 1024
        ),
    )(volume, coil_maps, kspace, line_mask, jnp.asarray(cos_table), jnp.asarray(sin_table))


def solution(mesh):
    return jax.shard_map(
        body,
        mesh=mesh,
        in_specs=(
            P(None, "cuts", "coil", None),
            P("coil", None, "cuts", None, None),
            P("coil", None, None, "cuts", None),
            P(),
        ),
        out_specs=P(None, "coil", "cuts", None),
        check_vma=False,
    )
```

profile of v0, /device:TPU:7, one launch (start us, length us, event | category | flops | bytes accessed | tf_op | source)
XLA Modules:
  0.0 154.3 jit_solution(7553037708588580547)
XLA Ops:
  0.0 152.6 %shard_map.64 = bf16[2,32,8,256]{3,2,1,0:T(8,128)(2,1)} custom-call(bf16[2,8,32,256]{3,2,1,0:T(8,128)(2,1)} %vol_in.1, bf16[2,2,8,256,256]{4,3,2,1,0:T(8,128)(2,1)} %maps_in.1, bf16[2,2,256,8,256]{4,3,2,1,0:T(8,128)(2,1)} %ks_in.1, s32[256,256]{1,0:T(8,128)} %mask_in.1, bf16[256,256]{1,0:T(8,128)(2,1)} %constant.4.clone.cos_in, ...), custom_call_target="tpu_custom_call" | custom-call | tf_op jit(solution)/shard_map/pallas_call | solution.py:337
  152.6 1.7 %copy.8 = bf16[2,32,8,256]{3,2,1,0:T(8,128)(2,1)} copy(bf16[2,32,8,256]{3,2,1,0:T(8,128)(2,1)} %shard_map.64) | data formatting | bytes 524288
where the time goes:
time: 154 us
  Pallas kernels  153 us (99%)
  local copies, waits for them, and re-layouts  1.67 us (1%)
    pallas_call x1, Pallas kernels, body(): pl.pallas_call(kernel, out_shape=jax.ShapeDtypeStruct((2, 32, 8, N), BF16...  153 us

commit v1 on v0

--- a/solution.py
+++ b/solution.py
@@ -1,4 +1,3 @@
-import functools
 import math
 
 import jax
@@ -15,8 +14,9 @@
 N = 256
 CUTS = 32
 PLANES = 8
-GROUPS = 4
-XP = PLANES // GROUPS
+SIZES = (2, 2, 2, 1, 1)
+GROUPS = len(SIZES)
+FIRST = tuple(sum(SIZES[:g]) for g in range(GROUPS))
 
 
 def tables():
@@ -36,16 +36,28 @@
 
 def kernel(
     vol_in, maps_in, ks_in, mask_in, cos_in, sin_in, out,
-    ks, maps, mask, vol, cosv, sinv, fwd, inv, split, merge, hyb, arr, kspc, gsend, rsbuf, psend, fin,
-    in_sem, vol_sem, agz_recv, agx_recv, ag_send, a2a_send, a2a_recv, rs_send, rs_recv, mv_send, mv_recv, mv_loc,
+    ks, maps, mask, vol, cosv, sinv, fwd, inv, split, merge, hyb, arr, kspc, gsend, rsbuf, psend, mid, osend, fin,
+    in_sem, vol_sem, agz_recv, agx_recv, ag_send, a2a_send, a2a_recv, rs_send, rs_recv, mid_send, mid_recv, mv_send, mv_recv, out_sem,
 ):
     me = lax.axis_index("cuts")
     my_coil = lax.axis_index("coil")
     zhi = lax.div(my_coil, 4)
     xpos = lax.rem(my_coil, 4)
     partner = lax.rem(my_coil + 4, 8)
-    home = lax.div(me, 4)
+    zlo = lax.div(me, 8)
+    ypos = lax.rem(lax.div(me, 2), 4)
+    core = lax.rem(me, 2)
     slot = lax.rem(me, 4)
+    shift = lax.rem(zlo + 2 * core, 4)
+    quarter = lax.rem(xpos + shift, 4)
+    mid_cut = quarter * 8 + lax.rem(me, 8)
+    mid_coil = lax.div(zlo, 2) * 4 + xpos
+    stays = jnp.logical_and(mid_cut == me, mid_coil == my_coil)
+    zlo_from = lax.rem(zlo + 8 - xpos - 2 * core, 4)
+    is_mid = lax.div(zlo_from, 2) == zhi
+    owner_coil = zlo_from * 2 + lax.div(ypos, 2)
+    keeps = owner_coil == my_coil
+    zlo_home = 2 * zhi + lax.div(xpos, 2)
 
     def load(k, src, dst):
         return pltpu.make_async_copy(src, dst, in_sem.at[k])
@@ -77,19 +89,23 @@
     greet(me, partner)
     for d in range(1, 4):
         greet(me, zhi * 4 + lax.rem(xpos + d, 4))
-    quarter = lax.div(me, 8)
-
-    def greet_source(k, carry):
-        a = my_coil * 4 + lax.rem(k, 4)
-        b = lax.div(k, 4) * 4 + quarter
+
+    @pl.when(is_mid)
+    def _():
+        for z in range(2):
+            a, b = zlo_from * 8 + lax.rem(me, 8), z * 4 + xpos
+
+            @pl.when(jnp.logical_or(a != me, b != my_coil))
+            def _():
+                greet(a, b)
+
+    for m in range(4):
+        a = zlo * 8 + lax.rem(xpos, 2) * 4 + m
+        b = zhi * 4 + lax.rem(zlo + 8 - zlo_home - 2 * (m % 2), 4)
 
         @pl.when(jnp.logical_or(a != me, b != my_coil))
         def _():
             greet(a, b)
-
-        return carry
-
-    lax.fori_loop(0, 8, greet_source, 0)
 
     loads[0].wait()
     loads[1].wait()
@@ -140,12 +156,12 @@
             lax.fori_loop(0, 8, gather, 0)
 
     def send_slabs(coil, group):
-        planes = pl.ds(group * XP, XP)
+        planes = pl.ds(FIRST[group], SIZES[group])
 
         def one(k, carry):
             to = lax.rem(me + k, CUTS)
             pltpu.make_async_remote_copy(
-                src_ref=hyb.at[coil, :, pl.ds(to * PLANES + group * XP, XP), :, :],
+                src_ref=hyb.at[coil, :, pl.ds(to * PLANES + FIRST[group], SIZES[group]), :, :],
                 dst_ref=arr.at[coil, :, planes, me, :, :],
                 send_sem=a2a_send.at[group],
                 recv_sem=a2a_recv.at[group],
@@ -156,7 +172,7 @@
 
         lax.fori_loop(1, CUTS, one, 0)
         pltpu.make_async_copy(
-            hyb.at[coil, :, pl.ds(me * PLANES + group * XP, XP), :, :],
+            hyb.at[coil, :, pl.ds(me * PLANES + FIRST[group], SIZES[group]), :, :],
             arr.at[coil, :, planes, me, :, :],
             a2a_recv.at[group],
         ).start()
@@ -173,7 +189,8 @@
 
     loads[2].wait()
     transform_x(0)
-    pl.semaphore_wait(barrier, 43 - self_count(me, my_coil))
+    greeted = jnp.where(is_mid, 8 - keeps.astype(jnp.int32), 0) + 1 - stays.astype(jnp.int32)
+    pl.semaphore_wait(barrier, 35 + greeted)
 
     send_volume(my_rows, vol_in, partner, agz_recv)
     for d in range(1, 4):
@@ -232,11 +249,11 @@
         return carry
 
     def send_sums(group):
-        planes = pl.ds(group * XP, XP)
+        planes = pl.ds(FIRST[group], SIZES[group])
         for d in range(1, 4):
             to = lax.rem(xpos + d, 4)
             pltpu.make_async_remote_copy(
-                src_ref=gsend.at[:, planes, pl.ds(pl.multiple_of(to * 64, 64), 64), :],
+                src_ref=gsend.at[:, planes, pl.ds(pl.multiple_of(lax.rem(to + shift, 4) * 64, 64), 64), :],
                 dst_ref=rsbuf.at[xpos, :, planes, :, :],
                 send_sem=rs_send.at[group],
                 recv_sem=rs_recv.at[group],
@@ -245,89 +262,126 @@
             ).start()
 
     lead = (1 - zhi).astype(F32)
-    own_rows = pl.ds(pl.multiple_of(xpos * 64, 64), 64)
+    own_rows = pl.ds(pl.multiple_of(quarter * 64, 64), 64)
 
     def finish_sums(group):
-        three = rsbuf.at[pl.ds(0, 3), :, pl.ds(group * XP, XP), :, :]
+        planes = pl.ds(FIRST[group], SIZES[group])
+        three = rsbuf.at[pl.ds(0, 3), :, planes, :, :]
         pltpu.make_async_copy(three, three, rs_recv.at[group]).wait()
 
         def one(t, carry):
             part = lax.rem(t, 2)
-            x = group * XP + lax.div(t, 2)
+            x = FIRST[group] + lax.div(t, 2)
             total = lead * vol[part, x, own_rows, :].astype(F32) + gsend[part, x, own_rows, :].astype(F32)
             for d in range(1, 4):
                 total += rsbuf[lax.rem(xpos + d, 4), part, x].astype(F32)
-            psend[part, x] = total.reshape(8, 8, N).astype(BF16)
+            psend[part, x] = total.astype(BF16)
             return carry
 
-        lax.fori_loop(0, 2 * XP, one, 0)
-
-        def move(k, carry):
-            to = xpos * 8 + k
-            src = psend.at[:, pl.ds(group * XP, XP), k, :, :]
-            dst = fin.at[zhi, :, pl.ds(slot * PLANES + group * XP, XP), :, :]
-            itself = jnp.logical_and(to == me, home == my_coil)
-
-            @pl.when(itself)
-            def _():
-                pltpu.make_async_copy(src, dst, mv_loc.at[group]).start()
-
-            @pl.when(jnp.logical_not(itself))
-            def _():
-                pltpu.make_async_remote_copy(
-                    src_ref=src,
-                    dst_ref=dst,
-                    send_sem=mv_send.at[group],
-                    recv_sem=mv_recv.at[group],
-                    device_id=(to, home),
-                    device_id_type=MESH,
-                ).start()
-
-            return carry
-
-        lax.fori_loop(0, 8, move, 0)
+        lax.fori_loop(0, 2 * SIZES[group], one, 0)
+        src = psend.at[:, planes, :, :]
+        dst = mid.at[zhi, :, planes, :, :]
+
+        @pl.when(stays)
+        def _():
+            pltpu.make_async_copy(src, dst, mid_recv.at[group]).start()
+
+        @pl.when(jnp.logical_not(stays))
+        def _():
+            pltpu.make_async_remote_copy(
+                src_ref=src,
+                dst_ref=dst,
+                send_sem=mid_send.at[group],
+                recv_sem=mid_recv.at[group],
+                device_id=(mid_cut, mid_coil),
+                device_id_type=MESH,
+            ).start()
+
+    def move_out(group):
+        planes = pl.ds(FIRST[group], SIZES[group])
+
+        @pl.when(is_mid)
+        def _():
+            both = mid.at[:, :, planes, :, :]
+            pltpu.make_async_copy(both, both, mid_recv.at[group]).wait()
+
+            def one(t, carry):
+                part = lax.rem(t, 2)
+                x = FIRST[group] + lax.div(t, 2)
+                total = mid[0, part, x].astype(F32) + mid[1, part, x].astype(F32)
+                osend[part, x] = total.reshape(8, 8, N).astype(BF16)
+                return carry
+
+            lax.fori_loop(0, 2 * SIZES[group], one, 0)
+
+            def move(k, carry):
+                src = osend.at[:, planes, k, :, :]
+                dst = fin.at[:, pl.ds(slot * PLANES + FIRST[group], SIZES[group]), :, :]
+                itself = jnp.logical_and(keeps, lax.rem(me, 8) == k)
+
+                @pl.when(itself)
+                def _():
+                    pltpu.make_async_copy(src, dst, mv_recv.at[group]).start()
+
+                @pl.when(jnp.logical_not(itself))
+                def _():
+                    pltpu.make_async_remote_copy(
+                        src_ref=src,
+                        dst_ref=dst,
+                        send_sem=mv_send.at[group],
+                        recv_sem=mv_recv.at[group],
+                        device_id=(zlo * 8 + k, owner_coil),
+                        device_id_type=MESH,
+                    ).start()
+
+                return carry
+
+            lax.fori_loop(0, 8, move, 0)
 
     for group in range(GROUPS):
-        here = arr.at[:, :, pl.ds(group * XP, XP), :, :, :]
+        here = arr.at[:, :, pl.ds(FIRST[group], SIZES[group]), :, :, :]
         pltpu.make_async_copy(here, here, a2a_recv.at[group]).wait()
-        lax.fori_loop(group * XP, (group + 1) * XP, back, 0)
+        lax.fori_loop(FIRST[group], FIRST[group] + SIZES[group], back, 0)
         send_sums(group)
         if group > 0:
             finish_sums(group - 1)
+        if group > 1:
+            move_out(group - 2)
+    move_out(GROUPS - 2)
     finish_sums(GROUPS - 1)
-
-    alone = self_count(me, my_coil) == 1
+    move_out(GROUPS - 1)
+
     for group in range(GROUPS):
-        full = psend.at[:, pl.ds(group * XP, XP), :, :, :]
-        most = psend.at[:, pl.ds(group * XP, XP), pl.ds(0, 7), :, :]
-        single = psend.at[:, pl.ds(group * XP, XP), 0, :, :]
-
-        @pl.when(alone)
-        def _():
-            pltpu.make_async_copy(most, most, mv_recv.at[group]).wait()
-            pltpu.make_async_copy(single, single, mv_loc.at[group]).wait()
-            pltpu.make_async_copy(most, most, mv_send.at[group]).wait()
-
-        @pl.when(jnp.logical_not(alone))
-        def _():
-            pltpu.make_async_copy(full, full, mv_recv.at[group]).wait()
-            pltpu.make_async_copy(full, full, mv_send.at[group]).wait()
-
-    for part in range(2):
-        out[part] = (fin[0, part].astype(F32) + fin[1, part].astype(F32)).astype(BF16)
+        four = fin.at[:, pl.ds(0, 4 * SIZES[group]), :, :]
+        pltpu.make_async_copy(four, four, mv_recv.at[group]).wait()
+    result = pltpu.make_async_copy(fin, out, out_sem)
+    result.start()
 
     for group in range(GROUPS):
-        sent = hyb.at[:, :, pl.ds(0, 31 * XP), :, :]
+        planes = pl.ds(FIRST[group], SIZES[group])
+        sent = hyb.at[:, :, pl.ds(0, 31 * SIZES[group]), :, :]
         pltpu.make_async_copy(sent, sent, a2a_send.at[group]).wait()
-        three = rsbuf.at[pl.ds(0, 3), :, pl.ds(group * XP, XP), :, :]
+        three = rsbuf.at[pl.ds(0, 3), :, planes, :, :]
         pltpu.make_async_copy(three, three, rs_send.at[group]).wait()
+
+        @pl.when(jnp.logical_not(stays))
+        def _():
+            part = psend.at[:, planes, :, :]
+            pltpu.make_async_copy(part, part, mid_send.at[group]).wait()
+
+        @pl.when(jnp.logical_and(is_mid, keeps))
+        def _():
+            seven = osend.at[:, planes, pl.ds(0, 7), :, :]
+            pltpu.make_async_copy(seven, seven, mv_send.at[group]).wait()
+
+        @pl.when(jnp.logical_and(is_mid, jnp.logical_not(keeps)))
+        def _():
+            eight = osend.at[:, planes, :, :, :]
+            pltpu.make_async_copy(eight, eight, mv_send.at[group]).wait()
+
     seven = vol.at[:, :, pl.ds(0, 224), :]
     pltpu.make_async_copy(seven, seven, ag_send).wait()
-
-
-def self_count(me, my_coil):
-    same = jnp.logical_and(lax.div(me, 8) == lax.rem(my_coil, 4), lax.div(me, 4) == my_coil)
-    return same.astype(jnp.int32)
+    result.wait()
 
 
 def body(volume, coil_maps, kspace, line_mask):
@@ -338,7 +392,7 @@
         kernel,
         out_shape=jax.ShapeDtypeStruct((2, 32, 8, N), BF16),
         in_specs=[any_space] * 6,
-        out_specs=pl.BlockSpec(memory_space=pltpu.VMEM),
+        out_specs=any_space,
         scratch_shapes=[
             pltpu.VMEM((2, 2, N, 8, N), BF16),
             pltpu.VMEM((2, 2, PLANES, N, N), BF16),
@@ -355,8 +409,10 @@
             pltpu.VMEM((2, PLANES, 2 * N, N), BF16),
             pltpu.VMEM((2, PLANES, N, N), BF16),
             pltpu.VMEM((4, 2, PLANES, 64, N), BF16),
+            pltpu.VMEM((2, PLANES, 64, N), BF16),
+            pltpu.VMEM((2, 2, PLANES, 64, N), BF16),
             pltpu.VMEM((2, PLANES, 8, 8, N), BF16),
-            pltpu.VMEM((2, 2, 32, 8, N), BF16),
+            pltpu.VMEM((2, 32, 8, N), BF16),
             dma((6,)),
             dma,
             dma,
@@ -369,6 +425,8 @@
             dma((GROUPS,)),
             dma((GROUPS,)),
             dma((GROUPS,)),
+            dma((GROUPS,)),
+            dma,
         ],
         compiler_params=pltpu.CompilerParams(
             collective_id=0, has_side_effects=True, vmem_limit_bytes=60 * 1024 * 1024

time: 154 us -> 141 us (0.916)
  the two profiles are of different devices: /device:TPU:7 before, /device:TPU:1 now
where the time goes in v1:
time: 141 us
  Pallas kernels  139 us (99%)
  local copies, waits for them, and re-layouts  1.67 us (1%)
    pallas_call x1, Pallas kernels, body(): pl.pallas_call(kernel, out_shape=jax.ShapeDtypeStruct((2, 32, 8, N), BF16...  139 us

profile of v1, /device:TPU:1, one launch (start us, length us, event | category | flops | bytes accessed | tf_op | source)
XLA Modules:
  0.0 140.7 jit_solution(4490555014009620514)
XLA Ops:
  0.0 139.0 %shard_map.64 = bf16[2,32,8,256]{3,2,1,0:T(8,128)(2,1)} custom-call(bf16[2,8,32,256]{3,2,1,0:T(8,128)(2,1)} %vol_in.1, bf16[2,2,8,256,256]{4,3,2,1,0:T(8,128)(2,1)} %maps_in.1, bf16[2,2,256,8,256]{4,3,2,1,0:T(8,128)(2,1)} %ks_in.1, s32[256,256]{1,0:T(8,128)} %mask_in.1, bf16[256,256]{1,0:T(8,128)(2,1)} %constant.4.clone.cos_in, ...), custom_call_target="tpu_custom_call" | custom-call | tf_op jit(solution)/shard_map/pallas_call | solution.py:391
  139.0 1.7 %copy.8 = bf16[2,32,8,256]{3,2,1,0:T(8,128)(2,1)} copy(bf16[2,32,8,256]{3,2,1,0:T(8,128)(2,1)} %shard_map.64) | data formatting | bytes 524288

commit v2 on v1

--- a/solution.py
+++ b/solution.py
@@ -14,7 +14,7 @@
 N = 256
 CUTS = 32
 PLANES = 8
-SIZES = (2, 2, 2, 1, 1)
+SIZES = (3, 3, 1, 1)
 GROUPS = len(SIZES)
 FIRST = tuple(sum(SIZES[:g]) for g in range(GROUPS))
 
@@ -316,7 +316,7 @@
 
             def move(k, carry):
                 src = osend.at[:, planes, k, :, :]
-                dst = fin.at[:, pl.ds(slot * PLANES + FIRST[group], SIZES[group]), :, :]
+                dst = out.at[:, pl.ds(slot * PLANES + FIRST[group], SIZES[group]), :, :]
                 itself = jnp.logical_and(keeps, lax.rem(me, 8) == k)
 
                 @pl.when(itself)
@@ -345,17 +345,13 @@
         send_sums(group)
         if group > 0:
             finish_sums(group - 1)
-        if group > 1:
-            move_out(group - 2)
-    move_out(GROUPS - 2)
     finish_sums(GROUPS - 1)
-    move_out(GROUPS - 1)
-
     for group in range(GROUPS):
-        four = fin.at[:, pl.ds(0, 4 * SIZES[group]), :, :]
+        move_out(group)
+
+    for group in range(GROUPS):
+        four = out.at[:, pl.ds(0, 4 * SIZES[group]), :, :]
         pltpu.make_async_copy(four, four, mv_recv.at[group]).wait()
-    result = pltpu.make_async_copy(fin, out, out_sem)
-    result.start()
 
     for group in range(GROUPS):
         planes = pl.ds(FIRST[group], SIZES[group])
@@ -381,7 +377,6 @@
 
     seven = vol.at[:, :, pl.ds(0, 224), :]
     pltpu.make_async_copy(seven, seven, ag_send).wait()
-    result.wait()
 
 
 def body(volume, coil_maps, kspace, line_mask):

time: 141 us -> 139 us (0.986)
  the two profiles are of different devices: /device:TPU:1 before, /device:TPU:231 now
where the time goes in v2:
time: 139 us
  Pallas kernels  138 us (99%)
  local copies, waits for them, and re-layouts  1.67 us (1%)
    pallas_call x1, Pallas kernels, body(): pl.pallas_call(kernel, out_shape=jax.ShapeDtypeStruct((2, 32, 8, N), BF16...  138 us

profile of v2, /device:TPU:231, one launch (start us, length us, event | category | flops | bytes accessed | tf_op | source)
XLA Modules:
  0.0 139.4 jit_solution(16270554056641231020)
XLA Ops:
  0.0 137.7 %shard_map.64 = bf16[2,32,8,256]{3,2,1,0:T(8,128)(2,1)} custom-call(bf16[2,8,32,256]{3,2,1,0:T(8,128)(2,1)} %vol_in.1, bf16[2,2,8,256,256]{4,3,2,1,0:T(8,128)(2,1)} %maps_in.1, bf16[2,2,256,8,256]{4,3,2,1,0:T(8,128)(2,1)} %ks_in.1, s32[256,256]{1,0:T(8,128)} %mask_in.1, bf16[256,256]{1,0:T(8,128)(2,1)} %constant.4.clone.cos_in, ...), custom_call_target="tpu_custom_call" | custom-call | tf_op jit(solution)/shard_map/pallas_call | solution.py:386
  137.7 1.7 %copy.8 = bf16[2,32,8,256]{3,2,1,0:T(8,128)(2,1)} copy(bf16[2,32,8,256]{3,2,1,0:T(8,128)(2,1)} %shard_map.64) | data formatting | bytes 524288

commit v3 on v2

--- a/solution.py
+++ b/solution.py
@@ -193,7 +193,7 @@
     pl.semaphore_wait(barrier, 35 + greeted)
 
     send_volume(my_rows, vol_in, partner, agz_recv)
-    for d in range(1, 4):
+    for d in (2, 1, 3):
         send_volume(my_rows, vol_in, zhi * 4 + lax.rem(xpos + d, 4), agx_recv)
     send_slabs(0, 0)
     loads[3].wait()
@@ -201,7 +201,7 @@
     send_slabs(1, 0)
     pltpu.make_async_copy(vol_in, vol_in, agz_recv).wait()
     far_rows = pl.ds(pl.multiple_of(partner * 32, 32), 32)
-    for d in range(1, 4):
+    for d in (2, 1, 3):
         send_volume(far_rows, vol.at[:, :, far_rows, :], zhi * 4 + lax.rem(xpos + d, 4), agx_recv)
     for group in range(1, GROUPS):
         send_slabs(0, group)
@@ -250,7 +250,7 @@
 
     def send_sums(group):
         planes = pl.ds(FIRST[group], SIZES[group])
-        for d in range(1, 4):
+        for d in (2, 1, 3):
             to = lax.rem(xpos + d, 4)
             pltpu.make_async_remote_copy(
                 src_ref=gsend.at[:, planes, pl.ds(pl.multiple_of(lax.rem(to + shift, 4) * 64, 64), 64), :],

time: 139 us -> 138 us (level)
  Pallas kernels: 138 us -> 136 us
    pallas_call x1, Pallas kernels: 138 us -> 136 us  [body(): pl.pallas_call(kernel, out_shape=jax.ShapeDtypeStruct((2, 32, 8, N), BF16...]
where the time goes in v3:
time: 138 us
  Pallas kernels  136 us (99%)
  local copies, waits for them, and re-layouts  1.67 us (1%)
    pallas_call x1, Pallas kernels, body(): pl.pallas_call(kernel, out_shape=jax.ShapeDtypeStruct((2, 32, 8, N), BF16...  136 us

profile of v3, /device:TPU:231, one launch (start us, length us, event | category | flops | bytes accessed | tf_op | source)
XLA Modules:
  0.0 138.0 jit_solution(1253896836759664348)
XLA Ops:
  0.0 136.3 %shard_map.64 = bf16[2,32,8,256]{3,2,1,0:T(8,128)(2,1)} custom-call(bf16[2,8,32,256]{3,2,1,0:T(8,128)(2,1)} %vol_in.1, bf16[2,2,8,256,256]{4,3,2,1,0:T(8,128)(2,1)} %maps_in.1, bf16[2,2,256,8,256]{4,3,2,1,0:T(8,128)(2,1)} %ks_in.1, s32[256,256]{1,0:T(8,128)} %mask_in.1, bf16[256,256]{1,0:T(8,128)(2,1)} %constant.4.clone.cos_in, ...), custom_call_target="tpu_custom_call" | custom-call | tf_op jit(solution)/shard_map/pallas_call | solution.py:386
  136.3 1.7 %copy.8 = bf16[2,32,8,256]{3,2,1,0:T(8,128)(2,1)} copy(bf16[2,32,8,256]{3,2,1,0:T(8,128)(2,1)} %shard_map.64) | data formatting | bytes 524288
